TPU v7x, 512 devices: a whole 4x4x16 slice. The times are simulated.
512 devices in a mesh: leaf: 128 (over z, y, core), rep: 4 (over x).
Axes of the slice: x: 4, y: 4, z: 16, core: 2. Of those that a mesh axis runs over, the one named last changes fastest.
Arguments:
- positions: float32 [3, 8192, 128], P(None, ('leaf', 'rep')), may hold values from -6 to 6
- density: float32 [3, 8192, 128], P(None, ('leaf', 'rep')), may hold values from -6 to 6
- near_offset: int32 [8192, 12], P(('leaf', 'rep')), may hold values from -2 to 2
- near_count: int32 [8192], P(('leaf', 'rep')), may hold values from 1 to 12
- inter_list: int32 [512, 189], P(('leaf', 'rep')), may hold values from 0 to 511
- operator_index: int32 [512, 189], P(('leaf', 'rep')), may hold values from 0 to 3
- lattice_index: int32 [512], P(('leaf', 'rep')), may hold values from 0 to 1
- up_weight: bfloat16 [512, 384], replicated, may hold values from -0.3125 to 0.3125
- m2l_operators: bfloat16 [4, 512, 512], replicated, may hold values from -0.0390625 to 0.0390625
- lattice_operators: bfloat16 [2, 512, 512], replicated, may hold values from -0.01171875 to 0.01171875
- down_weight: bfloat16 [384, 512], replicated, may hold values from -0.5 to 0.5
Outputs:
- velocity: float32 [3, 8192, 128], P(None, ('leaf', 'rep'))
Inputs may be any that keep to these rules, and one draw needn't show every extreme that they name: `near_offset`: leaf g's near source leaves are (g + offset) mod 8192; slots at or past near_count are unused.
All inputs are finite; a program needn't handle non-finite values.
Results may differ from a plain program's by a relative error of at most 0.02.
Values may be sent and summed in bfloat16 or wider, within the bound.
A program may use at most 64 MiB of HBM per device.

v0:
```python
import math

import jax
import jax.numpy as jnp
from jax import lax
from jax.sharding import PartitionSpec as P


def padded(shard, sides, width):
    for axis, dim in sides:
        size, length = (lax.axis_size(axis), shard.shape[dim])
        up = [(i, (i + 1) % size) for i in range(size)]
        down = [(j, i) for i, j in up]
        last = lax.slice_in_dim(shard, length - width, length, axis=dim)
        first = lax.slice_in_dim(shard, 0, width, axis=dim)
        before = lax.ppermute(last, axis, up)
        after = lax.ppermute(first, axis, down)
        shard = jnp.concatenate([before, shard, after], axis=dim)
    return shard


def stokes_tile(target, source_pos, source_force, live_slots):
    offsets_xyz = target[:, None, :, None] - source_pos[:, :, None, :]
    distance_sq = jnp.sum(offsets_xyz * offsets_xyz, axis=0) + 0.05
    inverse = lax.rsqrt(distance_sq)
    inverse_cube = inverse * inverse * inverse
    projected = jnp.sum(offsets_xyz * source_force[:, :, None, :], axis=0)
    kernel_terms = source_force[:, :, None, :] * inverse + offsets_xyz * (projected * inverse_cube)
    kernel_terms = kernel_terms * live_slots[None, :, None, None]
    return jnp.sum(kernel_terms, axis=(1, 3)) * (1.0 / (8.0 * math.pi))


def body(
    positions,
    density,
    near_offset,
    near_count,
    inter_list,
    operator_index,
    lattice_index,
    up_weight,
    m2l_operators,
    lattice_operators,
    down_weight,
):
    per_box = positions.shape[1]
    node_count = positions.shape[2]
    kind_count = m2l_operators.shape[0]
    stacked = jnp.concatenate([positions, density], axis=0)
    extended = padded(stacked.astype(jnp.bfloat16), ((("leaf", "rep"), 1),), per_box).astype(
        stacked.dtype
    )
    slot_range = jnp.arange(near_offset.shape[1], dtype=jnp.int32)

    def one_leaf(leaf_slot):
        target = positions[:, leaf_slot]
        source_slot = leaf_slot + near_offset[leaf_slot] + per_box
        sources = jnp.take(extended, source_slot, axis=1)
        live_slots = (slot_range < near_count[leaf_slot]).astype(jnp.float32)
        return stokes_tile(target, sources[:3], sources[3:], live_slots)

    near_part = lax.map(one_leaf, jnp.arange(per_box, dtype=jnp.int32))
    near_part = jnp.transpose(near_part, (1, 0, 2))
    damping = 1.0 / (1.0 + jnp.sum(positions * positions, axis=0))
    summed = jnp.sum(density * damping[None], axis=1).reshape(-1).astype(jnp.bfloat16)
    coarse = jnp.dot(up_weight, summed, preferred_element_type=jnp.float32).astype(jnp.bfloat16)
    coarse_row = coarse.reshape(1, -1)
    box_ids = inter_list[0]
    op_kinds = operator_index[0]
    kind_range = jnp.arange(kind_count, dtype=jnp.int32)
    selector = (op_kinds[None, :] == kind_range[:, None]).astype(jnp.float32)
    all_blocks = lax.all_gather(coarse_row, ("leaf", "rep"), axis=0, tiled=True)
    chosen = jnp.take(all_blocks, box_ids, axis=0).astype(jnp.float32)
    grouped_sum = jnp.dot(selector, chosen, precision=lax.Precision.HIGHEST)
    block_sum = jnp.sum(all_blocks.astype(jnp.float32), axis=0)
    block_sum = lax.psum(coarse.astype(jnp.float32), ("leaf", "rep"))
    total = block_sum.astype(jnp.bfloat16)
    grouped = grouped_sum.astype(jnp.bfloat16)
    local = jnp.einsum("tij,tj->i", m2l_operators, grouped, preferred_element_type=jnp.float32)
    local = local + jnp.dot(
        lattice_operators[lattice_index[0]], total, preferred_element_type=jnp.float32
    )
    local_bf = local.astype(jnp.bfloat16)
    far_part = jnp.dot(down_weight, local_bf, preferred_element_type=jnp.float32).reshape(
        3, node_count
    )
    return near_part + damping[None] * far_part[:, None, :]


def solution(mesh):
    in_specs = (
        P(None, ("leaf", "rep"), None),
        P(None, ("leaf", "rep"), None),
        P(("leaf", "rep"), None),
        P(("leaf", "rep")),
        P(("leaf", "rep"), None),
        P(("leaf", "rep"), None),
        P(("leaf", "rep")),
        P(),
        P(),
        P(),
        P(),
    )
    out_specs = P(None, ("leaf", "rep"), None)
    return jax.shard_map(body, mesh=mesh, in_specs=in_specs, out_specs=out_specs, check_vma=False)
```

profile of v0, /device:TPU:1, one launch (start us, length us, event | category | flops | bytes accessed | tf_op | source)
XLA Modules:
  0.0 413.2 jit_solution(9846070013614672958)
XLA Ops:
  0.0 0.9 multiply_reduce_fusion.1
  0.9 0.8 multiply_reduce_fusion
  1.8 3.9 collective-permute-start
  5.7 3.7 collective-permute-start.1
  9.5 1.2 fusion.22
  10.7 108.8 %psum.7 = bf16[512]{0:T(512)(128)(2,1)S(1)} all-reduce(bf16[512]{0:T(512)(128)(2,1)S(1)} %convert_element_type.40), channel_id=1, replica_groups=mesh['leaf'=128,'rep'=4] {'leaf','rep'}, use_global_device_ids=true, to_apply=%region_7.8 | all-reduce | flops 512 | bytes 2048 | tf_op jit(solution)/shard_map/psum | solution.py:76
  120.2 130.0 %all-gather.1 = bf16[512,1,512]{2,1,0:T(2,128)(2,1)S(1)} all-gather(bf16[1,1,512]{2,1,0:T(2,128)(2,1)S(1)} %reshape.142), channel_id=2, replica_groups=mesh['leaf'=128,'rep'=4] {'leaf','rep'}, dimensions={0}, use_global_device_ids=true | all-gather | bytes 525312 | tf_op jit(solution)/shard_map/all_gather | solution.py:72
  250.4 1.0 gather_fusion.1
  252.3 1.3 fusion.10
  254.0 158.6 %while.13 = (s32[]{:T(128)}, f32[16,3,128]{2,0,1:T(8,128)S(1)}, s32[16]{0:T(128)S(1)}, s32[16,12]{1,0:T(8,128)}, f32[6,48,128]{2,0,1:T(8,128)S(1)}, /*index=5*/f...) while((s32[]{:T(128)}, f32[16,3,128]{2,0,1:T(8,128)S(1)}, ...), condition=%wide.region_4.5_spmd.clone, body=%wide.region_0.4_spmd.clone.sunk | while | flops 6891705 | bytes 6684707 | solution.py:62
  256.8 1.4 fusion.33
  258.7 1.4 compare_and_fusion.3
  260.2 0.7 constant_dynamic-slice_fusion.2
  266.7 1.4 fusion.33
  268.6 1.4 compare_and_fusion.3
  270.1 0.7 constant_dynamic-slice_fusion.2
  272.4 0.7 compare_convert_fusion.2
  276.6 1.4 fusion.33
  278.5 1.4 compare_and_fusion.3
  280.1 0.7 constant_dynamic-slice_fusion.2
  286.5 1.4 fusion.33
  288.5 1.4 compare_and_fusion.3
  290.0 0.7 constant_dynamic-slice_fusion.2
  292.2 0.7 compare_convert_fusion.2
  296.4 1.4 fusion.33
  298.4 1.4 compare_and_fusion.3
  299.9 0.7 constant_dynamic-slice_fusion.2
  306.3 1.4 fusion.33
  308.3 1.4 compare_and_fusion.3
  309.8 0.7 constant_dynamic-slice_fusion.2
  316.2 1.4 fusion.33
  318.2 1.4 compare_and_fusion.3
  319.7 0.7 constant_dynamic-slice_fusion.2
  321.9 0.7 compare_convert_fusion.2
  326.1 1.4 fusion.33
  328.1 1.4 compare_and_fusion.3
  329.6 0.7 constant_dynamic-slice_fusion.2
  336.1 1.4 fusion.33
  338.0 1.4 compare_and_fusion.3
  339.5 0.7 constant_dynamic-slice_fusion.2
  341.8 0.7 compare_convert_fusion.2
  346.0 1.4 fusion.33
  347.9 1.4 compare_and_fusion.3
  349.5 0.7 constant_dynamic-slice_fusion.2
  355.9 1.4 fusion.33
  357.8 1.4 compare_and_fusion.3
  359.4 0.7 constant_dynamic-slice_fusion.2
  365.8 1.4 fusion.33
  367.8 1.4 compare_and_fusion.3
  369.3 0.7 constant_dynamic-slice_fusion.2
  375.7 1.4 fusion.33
  377.7 1.4 compare_and_fusion.3
  379.2 0.7 constant_dynamic-slice_fusion.2
  385.6 1.4 fusion.33
  387.6 1.4 compare_and_fusion.3
  389.1 0.7 constant_dynamic-slice_fusion.2
  391.3 0.7 compare_convert_fusion.2
  395.5 1.4 fusion.33
  397.5 1.4 compare_and_fusion.3
  399.0 0.7 constant_dynamic-slice_fusion.2
  405.4 1.4 fusion.33
  407.4 1.4 compare_and_fusion.3
  408.9 0.7 constant_dynamic-slice_fusion.2
  411.2 0.7 compare_convert_fusion.2
  (282 shorter events, 65.8 us)
Async XLA Ops:
  0.0 251.6 %copy-start = (bf16[4,512,512]{2,1,0:T(8,128)(2,1)S(1)}, bf16[4,512,512]{2,1,0:T(8,128)(2,1)}, u32[]{:S(2)}) copy-start(bf16[4,512,512]{2,1,0:T(8,128)(2,1)} %param.21) | copy-start | bytes 6291460
  0.0 250.3 %copy-start.2 = (s32[1,189]{1,0:T(1,128)S(1)}, s32[1,189]{1,0:T(1,128)}, u32[]{:S(2)}) copy-start(s32[1,189]{1,0:T(1,128)} %param.17) | copy-start | bytes 2272
  1.8 252.1 %collective-permute-start = (bf16[6,16,128]{2,1,0:T(8,128)(2,1)S(1)}, bf16[6,16,128]{2,1,0:T(8,128)(2,1)S(1)}, u32[]{:S(2)}, u32[]{:S(2)}) collective-permute-start(bf16[6,16,128]{2,1,0:T(8,128)(2,1)S(1)} %pad_maximum_fusion), channel_id=1, source_target_pairs={{0,1},{1,2},{2,3},{3,4},{4,5},{5,6},{6,7},{7,8},{8,9},{9,10},{10,1... | collective-permute-start | bytes 73736 | tf_op jit(solution)/shard_map/ppermute | solution.py:16
  5.7 248.2 %collective-permute-start.1 = (bf16[6,16,128]{2,1,0:T(8,128)(2,1)S(1)}, bf16[6,16,128]{2,1,0:T(8,128)(2,1)S(1)}, u32[]{:S(2)}, u32[]{:S(2)}) collective-permute-start(bf16[6,16,128]{2,1,0:T(8,128)(2,1)S(1)} %pad_maximum_fusion), channel_id=1, source_target_pairs={{1,0},{2,1},{3,2},{4,3},{5,4},{6,5},{7,6},{8,7},{9,8},{10,9},{11,1... | collective-permute-start | bytes 73736 | tf_op jit(solution)/shard_map/ppermute | solution.py:17
  120.2 131.2 %copy-start.3 = (s32[1,189]{1,0:T(1,128)S(1)}, s32[1,189]{1,0:T(1,128)}, u32[]{:S(2)}) copy-start(s32[1,189]{1,0:T(1,128)} %param.18) | copy-start | bytes 2272
  250.4 3.2 copy-start.1
  251.4 2.6 copy-start.4
where the time goes:
time: 420 us; the launch traced here: 413 us
  blocking collectives  239 us (57%)
  other arithmetic  83.3 us (20%)
  local copies, waits for them, and re-layouts  44.2 us (11%)
  loops' own time  34.7 us (8%)
  starting transfers between devices  7.7 us (2%)
    all_gather x1, blocking collectives, body(): all_blocks = lax.all_gather(coarse_row, ('leaf', 'rep'), axis=0, tiled=True)  130 us
    psum x1, blocking collectives, body(): block_sum = lax.psum(coarse.astype(jnp.float32), ('leaf', 'rep'))  109 us
    another operation x1, loops' own time, body(): near_part = lax.map(one_leaf, jnp.arange(per_box, dtype=jnp.int32))  34.7 us
    select_n x32, other arithmetic, one_leaf(): sources = jnp.take(extended, source_slot, axis=1)  23.5 us
    and x16, other arithmetic, one_leaf(): sources = jnp.take(extended, source_slot, axis=1)  22.2 us
    dynamic_slice x32, local copies, waits for them, and re-layouts, one_leaf(): target = positions[:, leaf_slot]  11.6 us
    convert_element_type x16, other arithmetic, one_leaf(): live_slots = (slot_range < near_count[leaf_slot]).astype(jnp.float32)  11 us
    reduce_sum x16, other arithmetic, stokes_tile(): return jnp.sum(kernel_terms, axis=(1, 3)) * (1.0 / (8.0 * math.pi))  10.7 us
  transfers between devices with their start and end apart: 2, of which 0 were waited for; matrix products, arithmetic and copies ran while one was open for 1% of the time, Pallas kernels for 0%

commit v1 on v0

v1 whole, which is shorter than its diff:
```python
import functools
import math

import jax
import jax.numpy as jnp
from jax import lax
from jax.experimental import pallas as pl
from jax.experimental.pallas import tpu as pltpu
from jax.sharding import PartitionSpec as P

MESH = pl.DeviceIdType.MESH
F32 = jnp.float32
BF16 = jnp.bfloat16
NT = (((1,), (1,)), ((), ()))


def dot_nt(a, b):
    return lax.dot_general(a, b, NT, preferred_element_type=F32)


def split3(v):
    hi = v.astype(BF16).astype(F32)
    rest = v - hi
    mid = rest.astype(BF16).astype(F32)
    return hi, mid, rest - mid


def kernel(
    dims,
    early,
    middle,
    pos_ref,
    den_ref,
    off_ref,
    cnt_ref,
    ids_ref,
    ops_ref,
    lat_idx_ref,
    up_hbm,
    m2l_hbm,
    lat_hbm,
    down_hbm,
    out_ref,
    up_v,
    m2l_v,
    lat_v,
    down_v,
    halo,
    id_s,
    op_s,
    csend,
    crecv,
    gz,
    stage,
    plane,
    psend,
    precv,
    b_s,
    a_s,
    l_s,
    at_s,
    m_s,
    acc_s,
    wsem,
    zsend,
    zrecv,
    xsend,
    xrecv,
    hsend,
    hrecv,
    osend,
    orecv,
):
    nz, ny, nx = dims
    planes = ny * nx
    per_z = 2 * ny
    leaf = lax.axis_index("leaf")
    rep = lax.axis_index("rep")
    z = leaf // per_z
    y = lax.rem(leaf // 2, ny)
    core = lax.rem(leaf, 2)
    box = leaf * nx + rep
    boxes = nz * ny * nx * 2
    me_p = y * nx + rep

    def z_peer(d):
        return (lax.rem(z + d, nz) * per_z + y * 2 + core, rep)

    def p_peer(d):
        return (
            z * per_z + lax.rem(y + d // nx, ny) * 2 + core,
            lax.rem(rep + lax.rem(d, nx), nx),
        )

    partner = (leaf + 1 - 2 * core, rep)
    after = lax.rem(box + 1, boxes)
    before = lax.rem(box + boxes - 1, boxes)
    after = (after // nx, lax.rem(after, nx))
    before = (before // nx, lax.rem(before, nx))

    loads = [
        pltpu.make_async_copy(src, dst, wsem.at[i])
        for i, (src, dst) in enumerate(
            [(up_hbm, up_v), (m2l_hbm, m2l_v), (lat_hbm, lat_v), (down_hbm, down_v)]
        )
    ]
    for load in loads:
        load.start()

    barrier = pltpu.get_barrier_semaphore()

    def greet(peer):
        pl.semaphore_signal(barrier, inc=1, device_id=peer, device_id_type=MESH)

    @pl.loop(1, nz)
    def _(d):
        greet(z_peer(d))

    @pl.loop(1, planes)
    def _(d):
        greet(p_peer(d))

    greet(partner)
    greet(after)
    greet(before)

    x = [pos_ref[c] for c in range(3)]
    f = [den_ref[c] for c in range(3)]
    x2 = x[0] * x[0] + x[1] * x[1] + x[2] * x[2]
    damping = 1.0 / (1.0 + x2)
    summed = jnp.concatenate(
        [jnp.sum(f[c] * damping, axis=0, keepdims=True) for c in range(3)], axis=1
    )
    summed = jnp.broadcast_to(summed, (8, summed.shape[1])).astype(BF16)
    loads[0].wait()
    coarse = dot_nt(summed, up_v[...]).astype(BF16).astype(F32)
    gz[z] = coarse[0:1]

    half = boxes // 2
    id_s[...] = jnp.full(id_s.shape, -1, jnp.int32)
    op_s[...] = jnp.full(op_s.shape, -1, jnp.int32)
    nil = ids_ref.shape[1]
    id_s[0:1, 0:nil] = ids_ref[...]
    op_s[0:1, 0:nil] = ops_ref[...]
    ids = id_s[0:1, :]
    kinds = op_s[0:1, :]
    sx, sy = nx.bit_length() - 1, ny.bit_length() - 1
    id_x = ids & (nx - 1)
    id_core = (ids >> sx) & 1
    id_y = (ids >> (sx + 1)) & (ny - 1)
    id_z = ids >> (sx + 1 + sy)
    column = jnp.where(ids < 0, -1, id_core * half + (id_y * nx + id_x) * nz + id_z)
    width = ids.shape[1]
    rows = lax.broadcasted_iota(jnp.int32, (boxes, width), 0)
    hot = jnp.where(rows == column, 1.0, 0.0).astype(BF16)
    kind_rows = lax.broadcasted_iota(jnp.int32, (8, width), 0)
    picks = jnp.where(kind_rows == kinds, 1.0, 0.0).astype(BF16)
    counts = dot_nt(picks, hot)
    one_row = lax.broadcasted_iota(jnp.int32, counts.shape, 0) == 4
    counts = jnp.where(one_row, 1.0, counts)
    left, right = counts[:, :half], counts[:, half:]
    first = core == 0
    csend[...] = jnp.where(first, right, left)
    own_counts = jnp.where(first, left, right)

    leaves = x2.shape[0]
    leaf_rows = lax.broadcasted_iota(jnp.int32, off_ref.shape, 0)
    slots = lax.broadcasted_iota(jnp.int32, off_ref.shape, 1)
    used = jnp.zeros(off_ref.shape, jnp.int32)
    for g in range(leaves):
        used = jnp.where(leaf_rows == g, cnt_ref[g], used)
    for o in range(5):
        hit = jnp.where((off_ref[...] == o - 2) & (slots < used), 1.0, 0.0)
        m_s[o] = jnp.broadcast_to(jnp.sum(hit, axis=1, keepdims=True), x2.shape)

    ones = jnp.ones(x2.shape, F32)
    zeros = jnp.zeros(x2.shape, F32)
    parts = [split3(v) for v in x]
    for s in range(3):
        for c in range(3):
            b_s[:, 3 * s + c, :] = parts[c][s]
    for s, v in enumerate(split3(x2 + 0.05)):
        b_s[:, 9 + s, :] = v
        b_s[:, 12 + s, :] = ones
    b_s[:, 15, :] = zeros

    def source_rows(lo, sx_, sf_):
        n = sx_[0].shape[0]
        at = pl.ds(lo, n)
        one, zero = jnp.ones(sx_[0].shape, F32), jnp.zeros(sx_[0].shape, F32)
        yy = [v.astype(BF16).astype(F32) for v in sx_]
        ff = [v.astype(BF16).astype(F32) for v in sf_]
        y2 = split3(yy[0] * yy[0] + yy[1] * yy[1] + yy[2] * yy[2])
        yf = split3(-(yy[0] * ff[0] + yy[1] * ff[1] + yy[2] * ff[2]))
        for s in range(3):
            for c in range(3):
                a_s[at, 3 * s + c, 0:128] = -2.0 * yy[c]
                a_s[at, 3 * s + c, 128:256] = ff[c]
            a_s[at, 9 + s, 0:128] = one
            a_s[at, 9 + s, 128:256] = zero
            a_s[at, 12 + s, 0:128] = y2[s]
            a_s[at, 12 + s, 128:256] = yf[s]
            l_s[at, s, 0:128] = ff[s]
            l_s[at, s, 128:256] = -yy[s]
        a_s[at, 15, 0:128] = zero
        a_s[at, 15, 128:256] = zero
        l_s[at, 3, 0:128] = zero
        l_s[at, 3, 128:256] = one
        for r in range(4, 8):
            l_s[at, r, 0:128] = zero
            l_s[at, r, 128:256] = zero

    def turn(lo, hi):
        @pl.loop(lo, hi)
        def _(i):
            at_s[i] = a_s[i].T.astype(BF16)

    source_rows(2, x, f)
    turn(2, leaves + 2)

    def near(lo, hi):
        @pl.loop(lo, hi)
        def _(g):
            target = b_s[g].astype(BF16)
            total = jnp.zeros((8, 128), F32)
            for o in range(5):
                qp = jnp.dot(at_s[g + o], target, preferred_element_type=F32)
                inv = lax.rsqrt(qp[0:128])
                w = qp[128:256] * (inv * inv * inv)
                pair = jnp.concatenate([inv, w], axis=0).astype(BF16)
                r = jnp.dot(l_s[g + o].astype(BF16), pair, preferred_element_type=F32)
                total = total + r * m_s[o, pl.ds(g, 1), :]
            acc_s[g] = total

    near(2, early)

    pl.semaphore_wait(barrier, nz + planes + 1)

    def z_copy(d):
        return pltpu.make_async_remote_copy(
            src_ref=gz.at[z],
            dst_ref=gz.at[z],
            send_sem=zsend.at[d],
            recv_sem=zrecv.at[d],
            device_id=z_peer(d),
            device_id_type=MESH,
        )

    def p_copy(d):
        return pltpu.make_async_remote_copy(
            src_ref=plane.at[me_p],
            dst_ref=plane.at[me_p],
            send_sem=xsend.at[d],
            recv_sem=xrecv.at[d],
            device_id=p_peer(d),
            device_id_type=MESH,
        )

    @pl.loop(1, nz)
    def _(d):
        z_copy(d).start()

    def remote(src, dst, s, r, peer):
        return pltpu.make_async_remote_copy(
            src_ref=src, dst_ref=dst, send_sem=s, recv_sem=r, device_id=peer, device_id_type=MESH
        )

    high = pl.ds(leaves - 8, 8)
    halos = [
        remote(pos_ref.at[:, high, :], halo.at[0], hsend.at[0], hrecv.at[0], after),
        remote(den_ref.at[:, high, :], halo.at[1], hsend.at[1], hrecv.at[1], after),
        remote(pos_ref.at[:, 0:8, :], halo.at[2], hsend.at[2], hrecv.at[2], before),
        remote(den_ref.at[:, 0:8, :], halo.at[3], hsend.at[3], hrecv.at[3], before),
    ]
    for copy in halos:
        copy.start()
    share = remote(csend, crecv, osend.at[0], orecv.at[0], partner)
    share.start()

    near(early, middle)

    @pl.loop(1, nz)
    def _(d):
        z_copy(d).wait_recv()

    for i in range(nz):
        stage[i : i + 1, :] = gz[i]
    plane[me_p] = stage[...].astype(BF16)

    @pl.loop(1, planes)
    def _(d):
        p_copy(d).start()

    near(middle, leaves - 2)
    for copy in halos:
        copy.wait_recv()
    source_rows(0, [halo[0, c, 6:8, :] for c in range(3)], [halo[1, c, 6:8, :] for c in range(3)])
    source_rows(
        leaves + 2, [halo[2, c, 0:2, :] for c in range(3)], [halo[3, c, 0:2, :] for c in range(3)]
    )
    turn(0, 2)
    turn(leaves + 2, leaves + 4)
    near(0, 2)
    near(leaves - 2, leaves)

    scale = 1.0 / (8.0 * math.pi)
    lever = acc_s[:, 3, :]
    near_part = [(acc_s[:, c, :] + x[c] * lever) * scale for c in range(3)]

    share.wait_recv()
    selector = jnp.concatenate([own_counts, crecv[...]], axis=0).astype(BF16)
    for load in loads[1:]:
        load.wait()

    @pl.loop(1, planes)
    def _(d):
        p_copy(d).wait_recv()

    blocks = plane[...].reshape(half, plane.shape[2])
    partial = jnp.dot(selector, blocks, preferred_element_type=F32)
    psend[...] = partial[8:16]
    swap = remote(psend, precv, osend.at[1], orecv.at[1], partner)
    swap.start()
    swap.wait_recv()
    grouped = (partial[0:8] + precv[...]).astype(BF16)

    def spread(t):
        return jnp.broadcast_to(grouped[t : t + 1].astype(F32), grouped.shape)

    lat_idx = lat_idx_ref[0]
    total = spread(4)
    local = jnp.zeros(grouped.shape, F32)
    for t in range(4):
        local = local + dot_nt(spread(t).astype(BF16), m2l_v[t])
    for i in range(2):
        kept = jnp.where(lat_idx == i, total, 0.0).astype(BF16)
        local = local + dot_nt(kept, lat_v[i])
    far = dot_nt(local.astype(BF16), down_v[...])
    for c in range(3):
        out_ref[c] = near_part[c] + damping * far[0:1, 128 * c : 128 * (c + 1)]

    @pl.loop(1, nz)
    def _(d):
        z_copy(d).wait_send()

    @pl.loop(1, planes)
    def _(d):
        p_copy(d).wait_send()

    for copy in halos + [share, swap]:
        copy.wait_send()


def body(dims, early, middle, pos, den, off, cnt, ids, ops, lat_idx, up, m2l, lat, down):
    nz, ny, nx = dims
    planes = ny * nx
    boxes = nz * planes * 2
    leaves = pos.shape[1]
    coef = up.shape[0]
    vm = pl.BlockSpec(memory_space=pltpu.VMEM)
    sm = pl.BlockSpec(memory_space=pltpu.SMEM)
    hbm = pl.BlockSpec(memory_space=pl.ANY)
    dma = pltpu.SemaphoreType.DMA
    return pl.pallas_call(
        functools.partial(kernel, dims, early, middle),
        out_shape=jax.ShapeDtypeStruct(pos.shape, F32),
        in_specs=[vm, vm, vm, sm, vm, vm, sm, hbm, hbm, hbm, hbm],
        out_specs=vm,
        scratch_shapes=[
            pltpu.VMEM(up.shape, BF16),
            pltpu.VMEM(m2l.shape, BF16),
            pltpu.VMEM(lat.shape, BF16),
            pltpu.VMEM(down.shape, BF16),
            pltpu.VMEM((4, 3, 8, 128), F32),
            pltpu.VMEM((8, 256), jnp.int32),
            pltpu.VMEM((8, 256), jnp.int32),
            pltpu.VMEM((8, boxes // 2), F32),
            pltpu.VMEM((8, boxes // 2), F32),
            pltpu.VMEM((nz, 1, coef), F32),
            pltpu.VMEM((nz, coef), F32),
            pltpu.VMEM((planes, nz, coef), BF16),
            pltpu.VMEM((8, coef), F32),
            pltpu.VMEM((8, coef), F32),
            pltpu.VMEM((leaves, 16, 128), F32),
            pltpu.VMEM((leaves + 4, 16, 256), F32),
            pltpu.VMEM((leaves + 4, 8, 256), F32),
            pltpu.VMEM((leaves + 4, 256, 16), BF16),
            pltpu.VMEM((5, leaves, 128), F32),
            pltpu.VMEM((leaves, 8, 128), F32),
            dma((4,)),
            dma((nz,)),
            dma((nz,)),
            dma((planes,)),
            dma((planes,)),
            dma((4,)),
            dma((4,)),
            dma((2,)),
            dma((2,)),
        ],
        compiler_params=pltpu.CompilerParams(
            collective_id=0, has_side_effects=True, vmem_limit_bytes=32 * 1024 * 1024
        ),
        name="fmm",
    )(pos, den, off, cnt, ids, ops, lat_idx, up, m2l, lat, down)


def solution(mesh):
    sizes = dict(mesh.shape)
    nx = sizes["rep"]
    ny = 4
    nz = sizes["leaf"] // (2 * ny)
    both = ("leaf", "rep")
    in_specs = (
        P(None, both, None),
        P(None, both, None),
        P(both, None),
        P(both),
        P(both, None),
        P(both, None),
        P(both),
        P(),
        P(),
        P(),
        P(),
    )
    run = functools.partial(body, (nz, ny, nx), 2, 14)
    return jax.shard_map(
        run, mesh=mesh, in_specs=in_specs, out_specs=P(None, both, None), check_vma=False
    )
```

time: 420 us -> 50.2 us (0.12); the launches traced: 413 us -> 49.8 us
  blocking collectives: 239 us -> 0 us
  other arithmetic: 83.3 us -> 0 us
  Pallas kernels: 0 us -> 39.5 us
  loops' own time: 34.7 us -> 0 us
  local copies, waits for them, and re-layouts: 44.2 us -> 9.59 us
  starting transfers between devices: 7.7 us -> 0 us
    all_gather x1 -> x0, blocking collectives: 130 us -> none  [body(): all_blocks = lax.all_gather(coarse_row, ('leaf', 'rep'), axis=0, tiled=True)]
    psum x1 -> x0, blocking collectives: 109 us -> none  [body(): block_sum = lax.psum(coarse.astype(jnp.float32), ('leaf', 'rep'))]
    pallas_call x0 -> x1, Pallas kernels: none -> 39.5 us  [body(): pl.pallas_call(functools.partial(kernel, dims, early, middle), out_shape=...]
    another operation x1 -> x0, loops' own time: 34.7 us -> none  [body(): near_part = lax.map(one_leaf, jnp.arange(per_box, dtype=jnp.int32))]
    dynamic_slice x64 -> x0, local copies, waits for them, and re-layouts: 33 us -> none  [the longest x32 11.6 us: one_leaf(): target = positions[:, leaf_slot]]
    select_n x33 -> x0, other arithmetic: 23.5 us -> none  [the longest x32 23.5 us: one_leaf(): sources = jnp.take(extended, source_slot, axis=1)]
    reduce_sum x34 -> x0, other arithmetic: 22.7 us -> none  [the longest x16 10.7 us: stokes_tile(): return jnp.sum(kernel_terms, axis=(1, 3)) * (1.0 / (8.0 * math.pi))]
    and x17 -> x0, other arithmetic: 22.3 us -> none  [the longest x16 22.2 us: one_leaf(): sources = jnp.take(extended, source_slot, axis=1)]
  transfers between devices with their start and end apart: 2 -> 0, of which waited for: 0 -> 0; matrix products, arithmetic and copies ran while one was open for 1% -> 0% of each run, Pallas kernels for 0% -> 0%
where the time goes in v1:
time: 50.2 us; the launch traced here: 49.8 us
  Pallas kernels  39.5 us (79%)
  local copies, waits for them, and re-layouts  9.59 us (19%)
  between operations  0.68 us (1%)
    pallas_call x1, Pallas kernels, body(): pl.pallas_call(functools.partial(kernel, dims, early, middle), out_shape=...  39.5 us
    unnamed x21, local copies, waits for them, and re-layouts  9.59 us

profile of v1, /device:TPU:1, one launch (start us, length us, event | category | flops | bytes accessed | tf_op | source)
XLA Modules:
  0.0 49.8 jit_solution(15617601989395176128)
XLA Ops:
  0.7 0.0 copy-start
  0.7 1.6 %copy-done = bf16[4,512,512]{2,1,0:T(8,128)(2,1)S(1)} copy-done((bf16[4,512,512]{2,1,0:T(8,128)(2,1)S(1)}, bf16[4,512,512]{2,1,0:T(8,128)(2,1)}, u32[]{:S(2)}) %copy-start) | copy-done | bytes 2097176
  2.2 0.0 copy-start.1
  2.2 1.2 %copy-done.1 = bf16[2,512,512]{2,1,0:T(8,128)(2,1)S(1)} copy-done((bf16[2,512,512]{2,1,0:T(8,128)(2,1)S(1)}, bf16[2,512,512]{2,1,0:T(8,128)(2,1)}, u32[]{:S(2)}) %copy-start.1) | copy-done | bytes 1048600
  3.5 0.0 copy-start.2
  3.5 1.0 %copy-done.2 = bf16[512,384]{1,0:T(8,128)(2,1)S(1)} copy-done((bf16[512,384]{1,0:T(8,128)(2,1)S(1)}, bf16[512,384]{1,0:T(8,128)(2,1)}, u32[]{:S(2)}) %copy-start.2) | copy-done | bytes 393240
  4.5 0.0 copy-start.3
  4.5 1.0 %copy-done.3 = bf16[384,512]{1,0:T(8,128)(2,1)S(1)} copy-done((bf16[384,512]{1,0:T(8,128)(2,1)S(1)}, bf16[384,512]{1,0:T(8,128)(2,1)}, u32[]{:S(2)}) %copy-start.3) | copy-done | bytes 393240
  5.5 0.0 copy-start.4
  5.5 0.7 %copy-done.4 = f32[3,16,128]{2,1,0:T(8,128)S(1)} copy-done((f32[3,16,128]{2,1,0:T(8,128)S(1)}, f32[3,16,128]{2,1,0:T(8,128)}, u32[]{:S(2)}) %copy-start.4) | copy-done | bytes 24600
  6.2 0.0 copy-start.5
  6.2 0.7 %copy-done.5 = f32[3,16,128]{2,1,0:T(8,128)S(1)} copy-done((f32[3,16,128]{2,1,0:T(8,128)S(1)}, f32[3,16,128]{2,1,0:T(8,128)}, u32[]{:S(2)}) %copy-start.5) | copy-done | bytes 24600
  6.9 0.0 copy-start.6
  6.9 0.7 %copy-done.6 = s32[16,12]{1,0:T(8,128)S(1)} copy-done((s32[16,12]{1,0:T(8,128)S(1)}, s32[16,12]{1,0:T(8,128)}, u32[]{:S(2)}) %copy-start.6) | copy-done | bytes 792
  7.6 0.0 copy-start.7
  7.6 0.7 %copy-done.7 = s32[1,189]{1,0:T(1,128)S(1)} copy-done((s32[1,189]{1,0:T(1,128)S(1)}, s32[1,189]{1,0:T(1,128)}, u32[]{:S(2)}) %copy-start.7) | copy-done | bytes 780
  8.3 0.0 copy-start.8
  8.3 0.7 %copy-done.8 = s32[1,189]{1,0:T(1,128)S(1)} copy-done((s32[1,189]{1,0:T(1,128)S(1)}, s32[1,189]{1,0:T(1,128)}, u32[]{:S(2)}) %copy-start.8) | copy-done | bytes 780
  9.0 0.0 copy-start.9
  9.0 0.7 %copy-done.9 = s32[16]{0:T(128)S(1)} copy-done((s32[16]{0:T(128)S(1)}, s32[16]{0:T(128)}, u32[]{:S(2)}) %copy-start.9) | copy-done | bytes 88
  9.7 39.5 %fmm.1 = f32[3,16,128]{2,1,0:T(8,128)S(1)} custom-call(f32[3,16,128]{2,1,0:T(8,128)S(1)} %copy-done.4, f32[3,16,128]{2,1,0:T(8,128)S(1)} %copy-done.5, s32[16,12]{1,0:T(8,128)S(1)} %copy-done.6, s32[16]{0:T(128)S(1)} %copy-done.9, s32[1,189]{1,0:T(1,128)S(1)} %copy-done.7, s32[1,189]{1,0:T(1,128)S(1)} %copy-done.8, s32[1]{0:T(128)S(6)} %copy.13.lat_idx_ref, ...), custom_call_target="tpu_custom_call" | custom-call | tf_op jit(solution)/shard_map/fmm/pallas_call | solution.py:364
  49.2 0.6 %copy.14 = f32[3,16,128]{2,1,0:T(8,128)} copy(f32[3,16,128]{2,1,0:T(8,128)S(1)} %fmm.1) | data formatting | bytes 49152
Async XLA Ops:
  0.7 1.6 %copy-start = (bf16[4,512,512]{2,1,0:T(8,128)(2,1)S(1)}, bf16[4,512,512]{2,1,0:T(8,128)(2,1)}, u32[]{:S(2)}) copy-start(bf16[4,512,512]{2,1,0:T(8,128)(2,1)} %m2l_hbm.1) | copy-start | bytes 6291460
  2.2 1.2 %copy-start.1 = (bf16[2,512,512]{2,1,0:T(8,128)(2,1)S(1)}, bf16[2,512,512]{2,1,0:T(8,128)(2,1)}, u32[]{:S(2)}) copy-start(bf16[2,512,512]{2,1,0:T(8,128)(2,1)} %lat_hbm.1) | copy-start | bytes 3145732
  3.5 1.0 %copy-start.2 = (bf16[512,384]{1,0:T(8,128)(2,1)S(1)}, bf16[512,384]{1,0:T(8,128)(2,1)}, u32[]{:S(2)}) copy-start(bf16[512,384]{1,0:T(8,128)(2,1)} %up_hbm.1) | copy-start | bytes 1179652
  4.5 1.0 %copy-start.3 = (bf16[384,512]{1,0:T(8,128)(2,1)S(1)}, bf16[384,512]{1,0:T(8,128)(2,1)}, u32[]{:S(2)}) copy-start(bf16[384,512]{1,0:T(8,128)(2,1)} %down_hbm.1) | copy-start | bytes 1179652
  5.5 0.7 %copy-start.4 = (f32[3,16,128]{2,1,0:T(8,128)S(1)}, f32[3,16,128]{2,1,0:T(8,128)}, u32[]{:S(2)}) copy-start(f32[3,16,128]{2,1,0:T(8,128)} %pos_ref.1) | copy-start | bytes 73732
  6.2 0.7 %copy-start.5 = (f32[3,16,128]{2,1,0:T(8,128)S(1)}, f32[3,16,128]{2,1,0:T(8,128)}, u32[]{:S(2)}) copy-start(f32[3,16,128]{2,1,0:T(8,128)} %den_ref.1) | copy-start | bytes 73732
  6.9 0.7 %copy-start.6 = (s32[16,12]{1,0:T(8,128)S(1)}, s32[16,12]{1,0:T(8,128)}, u32[]{:S(2)}) copy-start(s32[16,12]{1,0:T(8,128)} %off_ref.1) | copy-start | bytes 2308
  7.6 0.7 %copy-start.7 = (s32[1,189]{1,0:T(1,128)S(1)}, s32[1,189]{1,0:T(1,128)}, u32[]{:S(2)}) copy-start(s32[1,189]{1,0:T(1,128)} %ids_ref.1) | copy-start | bytes 2272
  8.3 0.7 %copy-start.8 = (s32[1,189]{1,0:T(1,128)S(1)}, s32[1,189]{1,0:T(1,128)}, u32[]{:S(2)}) copy-start(s32[1,189]{1,0:T(1,128)} %ops_ref.1) | copy-start | bytes 2272
  9.0 0.7 %copy-start.9 = (s32[16]{0:T(128)S(1)}, s32[16]{0:T(128)}, u32[]{:S(2)}) copy-start(s32[16]{0:T(128)} %cnt_ref.1) | copy-start | bytes 196

commit v2 on v1

--- a/solution.py
+++ b/solution.py
@@ -27,8 +27,18 @@
 
 def kernel(
     dims,
-    early,
-    middle,
+    pos_hbm,
+    den_hbm,
+    off_hbm,
+    cnt_hbm,
+    ids_hbm,
+    ops_hbm,
+    lat_idx_hbm,
+    up_hbm,
+    m2l_hbm,
+    lat_hbm,
+    down_hbm,
+    out_ref,
     pos_ref,
     den_ref,
     off_ref,
@@ -36,11 +46,6 @@
     ids_ref,
     ops_ref,
     lat_idx_ref,
-    up_hbm,
-    m2l_hbm,
-    lat_hbm,
-    down_hbm,
-    out_ref,
     up_v,
     m2l_v,
     lat_v,
@@ -101,20 +106,36 @@
     loads = [
         pltpu.make_async_copy(src, dst, wsem.at[i])
         for i, (src, dst) in enumerate(
-            [(up_hbm, up_v), (m2l_hbm, m2l_v), (lat_hbm, lat_v), (down_hbm, down_v)]
+            [
+                (pos_hbm, pos_ref),
+                (den_hbm, den_ref),
+                (up_hbm, up_v),
+                (ids_hbm, ids_ref),
+                (ops_hbm, ops_ref),
+                (off_hbm, off_ref),
+                (cnt_hbm, cnt_ref),
+                (lat_idx_hbm, lat_idx_ref),
+                (m2l_hbm, m2l_v),
+                (lat_hbm, lat_v),
+                (down_hbm, down_v),
+            ]
         )
     ]
-    for load in loads:
+    for load in loads[:8]:
         load.start()
 
+    leaves = pos_ref.shape[1]
     barrier = pltpu.get_barrier_semaphore()
 
     def greet(peer):
         pl.semaphore_signal(barrier, inc=1, device_id=peer, device_id_type=MESH)
 
-    @pl.loop(1, nz)
-    def _(d):
-        greet(z_peer(d))
+    def far_first(k):
+        return nz // 2 + ((k + 1) // 2) * (1 - 2 * lax.rem(k, 2))
+
+    @pl.loop(0, nz - 1)
+    def _(k):
+        greet(z_peer(far_first(k)))
 
     @pl.loop(1, planes)
     def _(d):
@@ -124,6 +145,8 @@
     greet(after)
     greet(before)
 
+    for load in loads[:2]:
+        load.wait()
     x = [pos_ref[c] for c in range(3)]
     f = [den_ref[c] for c in range(3)]
     x2 = x[0] * x[0] + x[1] * x[1] + x[2] * x[2]
@@ -132,11 +155,58 @@
         [jnp.sum(f[c] * damping, axis=0, keepdims=True) for c in range(3)], axis=1
     )
     summed = jnp.broadcast_to(summed, (8, summed.shape[1])).astype(BF16)
-    loads[0].wait()
+    loads[2].wait()
     coarse = dot_nt(summed, up_v[...]).astype(BF16).astype(F32)
     gz[z] = coarse[0:1]
 
+    pl.semaphore_wait(barrier, nz + planes + 1)
+
+    def z_copy(d):
+        return pltpu.make_async_remote_copy(
+            src_ref=gz.at[z],
+            dst_ref=gz.at[z],
+            send_sem=zsend.at[d],
+            recv_sem=zrecv.at[d],
+            device_id=z_peer(d),
+            device_id_type=MESH,
+        )
+
+    def p_copy(part, d):
+        return pltpu.make_async_remote_copy(
+            src_ref=plane.at[part, me_p],
+            dst_ref=plane.at[part, me_p],
+            send_sem=xsend.at[part, d],
+            recv_sem=xrecv.at[part, d],
+            device_id=p_peer(d),
+            device_id_type=MESH,
+        )
+
+    @pl.loop(0, nz - 1)
+    def _(k):
+        z_copy(far_first(k)).start()
+
+    def remote(src, dst, s, r, peer):
+        return pltpu.make_async_remote_copy(
+            src_ref=src, dst_ref=dst, send_sem=s, recv_sem=r, device_id=peer, device_id_type=MESH
+        )
+
+    high = pl.ds(leaves - 8, 8)
+    halos = [
+        remote(pos_ref.at[:, high, :], halo.at[0], hsend.at[0], hrecv.at[0], after),
+        remote(den_ref.at[:, high, :], halo.at[1], hsend.at[1], hrecv.at[1], after),
+        remote(pos_ref.at[:, 0:8, :], halo.at[2], hsend.at[2], hrecv.at[2], before),
+        remote(den_ref.at[:, 0:8, :], halo.at[3], hsend.at[3], hrecv.at[3], before),
+    ]
+    for copy in halos:
+        copy.start()
+    for load in loads[8:]:
+        load.start()
+
+    for load in loads[3:7]:
+        load.wait()
     half = boxes // 2
+    group, quarter = nz // 2, nz // 4
+    gb = group.bit_length() - 1
     id_s[...] = jnp.full(id_s.shape, -1, jnp.int32)
     op_s[...] = jnp.full(op_s.shape, -1, jnp.int32)
     nil = ids_ref.shape[1]
@@ -149,7 +219,9 @@
     id_core = (ids >> sx) & 1
     id_y = (ids >> (sx + 1)) & (ny - 1)
     id_z = ids >> (sx + 1 + sy)
-    column = jnp.where(ids < 0, -1, id_core * half + (id_y * nx + id_x) * nz + id_z)
+    slot = (id_z - z + quarter) & (nz - 1)
+    column = (slot >> gb) * (planes * group) + (id_y * nx + id_x) * group + (slot & (group - 1))
+    column = jnp.where(ids < 0, -1, id_core * half + column)
     width = ids.shape[1]
     rows = lax.broadcasted_iota(jnp.int32, (boxes, width), 0)
     hot = jnp.where(rows == column, 1.0, 0.0).astype(BF16)
@@ -162,8 +234,9 @@
     first = core == 0
     csend[...] = jnp.where(first, right, left)
     own_counts = jnp.where(first, left, right)
-
-    leaves = x2.shape[0]
+    share = remote(csend, crecv, osend.at[0], orecv.at[0], partner)
+    share.start()
+
     leaf_rows = lax.broadcasted_iota(jnp.int32, off_ref.shape, 0)
     slots = lax.broadcasted_iota(jnp.int32, off_ref.shape, 1)
     used = jnp.zeros(off_ref.shape, jnp.int32)
@@ -232,66 +305,26 @@
                 total = total + r * m_s[o, pl.ds(g, 1), :]
             acc_s[g] = total
 
-    near(2, early)
-
-    pl.semaphore_wait(barrier, nz + planes + 1)
-
-    def z_copy(d):
-        return pltpu.make_async_remote_copy(
-            src_ref=gz.at[z],
-            dst_ref=gz.at[z],
-            send_sem=zsend.at[d],
-            recv_sem=zrecv.at[d],
-            device_id=z_peer(d),
-            device_id_type=MESH,
-        )
-
-    def p_copy(d):
-        return pltpu.make_async_remote_copy(
-            src_ref=plane.at[me_p],
-            dst_ref=plane.at[me_p],
-            send_sem=xsend.at[d],
-            recv_sem=xrecv.at[d],
-            device_id=p_peer(d),
-            device_id_type=MESH,
-        )
-
-    @pl.loop(1, nz)
-    def _(d):
-        z_copy(d).start()
-
-    def remote(src, dst, s, r, peer):
-        return pltpu.make_async_remote_copy(
-            src_ref=src, dst_ref=dst, send_sem=s, recv_sem=r, device_id=peer, device_id_type=MESH
-        )
-
-    high = pl.ds(leaves - 8, 8)
-    halos = [
-        remote(pos_ref.at[:, high, :], halo.at[0], hsend.at[0], hrecv.at[0], after),
-        remote(den_ref.at[:, high, :], halo.at[1], hsend.at[1], hrecv.at[1], after),
-        remote(pos_ref.at[:, 0:8, :], halo.at[2], hsend.at[2], hrecv.at[2], before),
-        remote(den_ref.at[:, 0:8, :], halo.at[3], hsend.at[3], hrecv.at[3], before),
-    ]
-    for copy in halos:
-        copy.start()
-    share = remote(csend, crecv, osend.at[0], orecv.at[0], partner)
-    share.start()
-
-    near(early, middle)
-
-    @pl.loop(1, nz)
-    def _(d):
-        z_copy(d).wait_recv()
-
-    for i in range(nz):
-        stage[i : i + 1, :] = gz[i]
-    plane[me_p] = stage[...].astype(BF16)
-
-    @pl.loop(1, planes)
-    def _(d):
-        p_copy(d).start()
-
-    near(middle, leaves - 2)
+    near(2, leaves - 2)
+
+    def forward(part):
+        for i in range(group):
+            stage[i : i + 1, :] = gz[lax.rem(z + part * group + i - quarter + nz, nz)]
+        plane[part, me_p] = stage[...].astype(BF16)
+
+        @pl.loop(1, planes)
+        def _(d):
+            p_copy(part, d).start()
+
+    def z_wait(lo, hi):
+        @pl.loop(lo, hi)
+        def _(d):
+            z_copy(d).wait_recv()
+
+    z_wait(1, quarter + 1)
+    z_wait(nz - quarter + 1, nz)
+    forward(0)
+
     for copy in halos:
         copy.wait_recv()
     source_rows(0, [halo[0, c, 6:8, :] for c in range(3)], [halo[1, c, 6:8, :] for c in range(3)])
@@ -309,15 +342,23 @@
 
     share.wait_recv()
     selector = jnp.concatenate([own_counts, crecv[...]], axis=0).astype(BF16)
-    for load in loads[1:]:
+    for load in loads[7:]:
         load.wait()
 
-    @pl.loop(1, planes)
-    def _(d):
-        p_copy(d).wait_recv()
-
-    blocks = plane[...].reshape(half, plane.shape[2])
-    partial = jnp.dot(selector, blocks, preferred_element_type=F32)
+    z_wait(quarter + 1, nz - quarter + 1)
+    forward(1)
+
+    def gathered(part):
+        @pl.loop(1, planes)
+        def _(d):
+            p_copy(part, d).wait_recv()
+
+        n = planes * group
+        blocks = plane[part].reshape(n, plane.shape[3])
+        return jnp.dot(selector[:, part * n : (part + 1) * n], blocks, preferred_element_type=F32)
+
+    partial = gathered(0)
+    partial = partial + gathered(1)
     psend[...] = partial[8:16]
     swap = remote(psend, precv, osend.at[1], orecv.at[1], partner)
     swap.start()
@@ -345,28 +386,35 @@
 
     @pl.loop(1, planes)
     def _(d):
-        p_copy(d).wait_send()
+        p_copy(0, d).wait_send()
+        p_copy(1, d).wait_send()
 
     for copy in halos + [share, swap]:
         copy.wait_send()
 
 
-def body(dims, early, middle, pos, den, off, cnt, ids, ops, lat_idx, up, m2l, lat, down):
+def body(dims, pos, den, off, cnt, ids, ops, lat_idx, up, m2l, lat, down):
     nz, ny, nx = dims
     planes = ny * nx
     boxes = nz * planes * 2
     leaves = pos.shape[1]
     coef = up.shape[0]
     vm = pl.BlockSpec(memory_space=pltpu.VMEM)
-    sm = pl.BlockSpec(memory_space=pltpu.SMEM)
-    hbm = pl.BlockSpec(memory_space=pl.ANY)
+    hbm = pl.BlockSpec(memory_space=pltpu.HBM)
     dma = pltpu.SemaphoreType.DMA
     return pl.pallas_call(
-        functools.partial(kernel, dims, early, middle),
+        functools.partial(kernel, dims),
         out_shape=jax.ShapeDtypeStruct(pos.shape, F32),
-        in_specs=[vm, vm, vm, sm, vm, vm, sm, hbm, hbm, hbm, hbm],
+        in_specs=[hbm] * 11,
         out_specs=vm,
         scratch_shapes=[
+            pltpu.VMEM(pos.shape, F32),
+            pltpu.VMEM(den.shape, F32),
+            pltpu.VMEM(off.shape, jnp.int32),
+            pltpu.SMEM(cnt.shape, jnp.int32),
+            pltpu.VMEM(ids.shape, jnp.int32),
+            pltpu.VMEM(ops.shape, jnp.int32),
+            pltpu.SMEM(lat_idx.shape, jnp.int32),
             pltpu.VMEM(up.shape, BF16),
             pltpu.VMEM(m2l.shape, BF16),
             pltpu.VMEM(lat.shape, BF16),
@@ -377,8 +425,8 @@
             pltpu.VMEM((8, boxes // 2), F32),
             pltpu.VMEM((8, boxes // 2), F32),
             pltpu.VMEM((nz, 1, coef), F32),
-            pltpu.VMEM((nz, coef), F32),
-            pltpu.VMEM((planes, nz, coef), BF16),
+            pltpu.VMEM((nz // 2, coef), F32),
+            pltpu.VMEM((2, planes, nz // 2, coef), BF16),
             pltpu.VMEM((8, coef), F32),
             pltpu.VMEM((8, coef), F32),
             pltpu.VMEM((leaves, 16, 128), F32),
@@ -387,18 +435,18 @@
             pltpu.VMEM((leaves + 4, 256, 16), BF16),
             pltpu.VMEM((5, leaves, 128), F32),
             pltpu.VMEM((leaves, 8, 128), F32),
-            dma((4,)),
+            dma((11,)),
             dma((nz,)),
             dma((nz,)),
-            dma((planes,)),
-            dma((planes,)),
+            dma((2, planes)),
+            dma((2, planes)),
             dma((4,)),
             dma((4,)),
             dma((2,)),
             dma((2,)),
         ],
         compiler_params=pltpu.CompilerParams(
-            collective_id=0, has_side_effects=True, vmem_limit_bytes=32 * 1024 * 1024
+            collective_id=0, has_side_effects=True, vmem_limit_bytes=67043328
         ),
         name="fmm",
     )(pos, den, off, cnt, ids, ops, lat_idx, up, m2l, lat, down)
@@ -423,7 +471,7 @@
         P(),
         P(),
     )
-    run = functools.partial(body, (nz, ny, nx), 2, 14)
+    run = functools.partial(body, (nz, ny, nx))
     return jax.shard_map(
         run, mesh=mesh, in_specs=in_specs, out_specs=P(None, both, None), check_vma=False
     )

time: 50.2 us -> 47.3 us (0.942)
  local copies, waits for them, and re-layouts: 9.59 us -> 1.35 us
  Pallas kernels: 39.5 us -> 45.1 us
    unnamed x21 -> x1, local copies, waits for them, and re-layouts: 9.59 us -> 1.35 us
    pallas_call x1, Pallas kernels: 39.5 us -> 45.1 us  [body(): pl.pallas_call(functools.partial(kernel, dims), out_shape=jax.ShapeDtypeS...]
where the time goes in v2:
time: 47.3 us; the launch traced here: 47.1 us
  Pallas kernels  45.1 us (95%)
  local copies, waits for them, and re-layouts  1.35 us (3%)
  between operations  0.66 us (1%)
    pallas_call x1, Pallas kernels, body(): pl.pallas_call(functools.partial(kernel, dims), out_shape=jax.ShapeDtypeS...  45.1 us
    unnamed x1, local copies, waits for them, and re-layouts  1.35 us

profile of v2, /device:TPU:1, one launch (start us, length us, event | category | flops | bytes accessed | tf_op | source)
XLA Modules:
  0.0 47.1 jit_solution(2342494706535895429)
XLA Ops:
  0.7 45.1 %fmm.1 = f32[3,16,128]{2,1,0:T(8,128)} custom-call(f32[3,16,128]{2,1,0:T(8,128)} %pos_hbm.1, f32[3,16,128]{2,1,0:T(8,128)} %den_hbm.1, s32[16,12]{1,0:T(8,128)} %off_hbm.1, s32[16]{0:T(128)} %cnt_hbm.1, s32[1,189]{1,0:T(1,128)} %ids_hbm.1, s32[1,189]{1,0:T(1,128)} %ops_hbm.1, s32[1]{0:T(128)S(6)} %copy.13.lat_idx_hbm, bf16[512,384]{1,0:T(8,128)(2,1)} %up_hbm.1, ...), custom_call_target="tpu_custom_call" | custom-call | tf_op jit(solution)/shard_map/fmm/pallas_call | solution.py:405
  45.8 1.3 %copy.14 = f32[3,16,128]{2,1,0:T(8,128)} copy(f32[3,16,128]{2,1,0:T(8,128)} %fmm.1) | data formatting | bytes 49152

commit v3 on v2

--- a/solution.py
+++ b/solution.py
@@ -27,6 +27,7 @@
 
 def kernel(
     dims,
+    ahead,
     pos_hbm,
     den_hbm,
     off_hbm,
@@ -159,6 +160,88 @@
     coarse = dot_nt(summed, up_v[...]).astype(BF16).astype(F32)
     gz[z] = coarse[0:1]
 
+    def source_rows(lo, sx_, sf_):
+        n = sx_[0].shape[0]
+        at = pl.ds(lo, n)
+        one, zero = jnp.ones(sx_[0].shape, F32), jnp.zeros(sx_[0].shape, F32)
+        yy = [v.astype(BF16).astype(F32) for v in sx_]
+        ff = [v.astype(BF16).astype(F32) for v in sf_]
+        y2 = split3(yy[0] * yy[0] + yy[1] * yy[1] + yy[2] * yy[2])
+        yf = split3(-(yy[0] * ff[0] + yy[1] * ff[1] + yy[2] * ff[2]))
+        for s in range(3):
+            for c in range(3):
+                a_s[at, 3 * s + c, 0:128] = -2.0 * yy[c]
+                a_s[at, 3 * s + c, 128:256] = ff[c]
+            a_s[at, 9 + s, 0:128] = one
+            a_s[at, 9 + s, 128:256] = zero
+            a_s[at, 12 + s, 0:128] = y2[s]
+            a_s[at, 12 + s, 128:256] = yf[s]
+            l_s[at, s, 0:128] = ff[s]
+            l_s[at, s, 128:256] = -yy[s]
+        a_s[at, 15, 0:128] = zero
+        a_s[at, 15, 128:256] = zero
+        l_s[at, 3, 0:128] = zero
+        l_s[at, 3, 128:256] = one
+        for r in range(4, 8):
+            l_s[at, r, 0:128] = zero
+            l_s[at, r, 128:256] = zero
+
+    def turn(lo, hi):
+        @pl.loop(lo, hi)
+        def _(i):
+            at_s[i] = a_s[i].T.astype(BF16)
+
+    def near(lo, hi):
+        @pl.loop(lo, hi)
+        def _(j):
+            g = 2 * j
+            pair = [b_s[g].astype(BF16), b_s[g + 1].astype(BF16)]
+            both = jnp.concatenate(pair, axis=1)
+            totals = [jnp.zeros((8, 128), F32)] * 2
+            for o in range(6):
+                used_by = [t for t in range(2) if 0 <= o - t < 5]
+                target = both if len(used_by) == 2 else pair[used_by[0]]
+                qp = jnp.dot(at_s[g + o], target, preferred_element_type=F32)
+                inv = lax.rsqrt(qp[0:128])
+                w = qp[128:256] * (inv * inv * inv)
+                terms = jnp.concatenate([inv, w], axis=0).astype(BF16)
+                r = jnp.dot(l_s[g + o].astype(BF16), terms, preferred_element_type=F32)
+                for i, t in enumerate(used_by):
+                    weight = m_s[o - t, pl.ds(g + t, 1), :]
+                    totals[t] = totals[t] + r[:, 128 * i : 128 * (i + 1)] * weight
+            acc_s[g] = totals[0]
+            acc_s[g + 1] = totals[1]
+
+    def inner():
+        for load in loads[5:7]:
+            load.wait()
+        leaf_rows = lax.broadcasted_iota(jnp.int32, off_ref.shape, 0)
+        slots = lax.broadcasted_iota(jnp.int32, off_ref.shape, 1)
+        used = jnp.zeros(off_ref.shape, jnp.int32)
+        for g in range(leaves):
+            used = jnp.where(leaf_rows == g, cnt_ref[g], used)
+        for o in range(5):
+            hit = jnp.where((off_ref[...] == o - 2) & (slots < used), 1.0, 0.0)
+            m_s[o] = jnp.broadcast_to(jnp.sum(hit, axis=1, keepdims=True), x2.shape)
+
+        ones = jnp.ones(x2.shape, F32)
+        zeros = jnp.zeros(x2.shape, F32)
+        parts = [split3(v) for v in x]
+        for s in range(3):
+            for c in range(3):
+                b_s[:, 3 * s + c, :] = parts[c][s]
+        for s, v in enumerate(split3(x2 + 0.05)):
+            b_s[:, 9 + s, :] = v
+            b_s[:, 12 + s, :] = ones
+        b_s[:, 15, :] = zeros
+        source_rows(2, x, f)
+        turn(2, leaves + 2)
+        near(1, leaves // 2 - 1)
+
+    @pl.when(z < ahead)
+    def _():
+        inner()
+
     pl.semaphore_wait(barrier, nz + planes + 1)
 
     def z_copy(d):
@@ -202,7 +285,7 @@
     for load in loads[8:]:
         load.start()
 
-    for load in loads[3:7]:
+    for load in loads[3:5]:
         load.wait()
     half = boxes // 2
     group, quarter = nz // 2, nz // 4
@@ -237,75 +320,10 @@
     share = remote(csend, crecv, osend.at[0], orecv.at[0], partner)
     share.start()
 
-    leaf_rows = lax.broadcasted_iota(jnp.int32, off_ref.shape, 0)
-    slots = lax.broadcasted_iota(jnp.int32, off_ref.shape, 1)
-    used = jnp.zeros(off_ref.shape, jnp.int32)
-    for g in range(leaves):
-        used = jnp.where(leaf_rows == g, cnt_ref[g], used)
-    for o in range(5):
-        hit = jnp.where((off_ref[...] == o - 2) & (slots < used), 1.0, 0.0)
-        m_s[o] = jnp.broadcast_to(jnp.sum(hit, axis=1, keepdims=True), x2.shape)
-
-    ones = jnp.ones(x2.shape, F32)
-    zeros = jnp.zeros(x2.shape, F32)
-    parts = [split3(v) for v in x]
-    for s in range(3):
-        for c in range(3):
-            b_s[:, 3 * s + c, :] = parts[c][s]
-    for s, v in enumerate(split3(x2 + 0.05)):
-        b_s[:, 9 + s, :] = v
-        b_s[:, 12 + s, :] = ones
-    b_s[:, 15, :] = zeros
-
-    def source_rows(lo, sx_, sf_):
-        n = sx_[0].shape[0]
-        at = pl.ds(lo, n)
-        one, zero = jnp.ones(sx_[0].shape, F32), jnp.zeros(sx_[0].shape, F32)
-        yy = [v.astype(BF16).astype(F32) for v in sx_]
-        ff = [v.astype(BF16).astype(F32) for v in sf_]
-        y2 = split3(yy[0] * yy[0] + yy[1] * yy[1] + yy[2] * yy[2])
-        yf = split3(-(yy[0] * ff[0] + yy[1] * ff[1] + yy[2] * ff[2]))
-        for s in range(3):
-            for c in range(3):
-                a_s[at, 3 * s + c, 0:128] = -2.0 * yy[c]
-                a_s[at, 3 * s + c, 128:256] = ff[c]
-            a_s[at, 9 + s, 0:128] = one
-            a_s[at, 9 + s, 128:256] = zero
-            a_s[at, 12 + s, 0:128] = y2[s]
-            a_s[at, 12 + s, 128:256] = yf[s]
-            l_s[at, s, 0:128] = ff[s]
-            l_s[at, s, 128:256] = -yy[s]
-        a_s[at, 15, 0:128] = zero
-        a_s[at, 15, 128:256] = zero
-        l_s[at, 3, 0:128] = zero
-        l_s[at, 3, 128:256] = one
-        for r in range(4, 8):
-            l_s[at, r, 0:128] = zero
-            l_s[at, r, 128:256] = zero
-
-    def turn(lo, hi):
-        @pl.loop(lo, hi)
-        def _(i):
-            at_s[i] = a_s[i].T.astype(BF16)
-
-    source_rows(2, x, f)
-    turn(2, leaves + 2)
-
-    def near(lo, hi):
-        @pl.loop(lo, hi)
-        def _(g):
-            target = b_s[g].astype(BF16)
-            total = jnp.zeros((8, 128), F32)
-            for o in range(5):
-                qp = jnp.dot(at_s[g + o], target, preferred_element_type=F32)
-                inv = lax.rsqrt(qp[0:128])
-                w = qp[128:256] * (inv * inv * inv)
-                pair = jnp.concatenate([inv, w], axis=0).astype(BF16)
-                r = jnp.dot(l_s[g + o].astype(BF16), pair, preferred_element_type=F32)
-                total = total + r * m_s[o, pl.ds(g, 1), :]
-            acc_s[g] = total
-
-    near(2, leaves - 2)
+    @pl.when(z >= ahead)
+    def _():
+        inner()
+
 
     def forward(part):
         for i in range(group):
@@ -333,8 +351,8 @@
     )
     turn(0, 2)
     turn(leaves + 2, leaves + 4)
-    near(0, 2)
-    near(leaves - 2, leaves)
+    near(0, 1)
+    near(leaves // 2 - 1, leaves // 2)
 
     scale = 1.0 / (8.0 * math.pi)
     lever = acc_s[:, 3, :]
@@ -393,7 +411,7 @@
         copy.wait_send()
 
 
-def body(dims, pos, den, off, cnt, ids, ops, lat_idx, up, m2l, lat, down):
+def body(dims, ahead, pos, den, off, cnt, ids, ops, lat_idx, up, m2l, lat, down):
     nz, ny, nx = dims
     planes = ny * nx
     boxes = nz * planes * 2
@@ -403,7 +421,7 @@
     hbm = pl.BlockSpec(memory_space=pltpu.HBM)
     dma = pltpu.SemaphoreType.DMA
     return pl.pallas_call(
-        functools.partial(kernel, dims),
+        functools.partial(kernel, dims, ahead),
         out_shape=jax.ShapeDtypeStruct(pos.shape, F32),
         in_specs=[hbm] * 11,
         out_specs=vm,
@@ -471,7 +489,7 @@
         P(),
         P(),
     )
-    run = functools.partial(body, (nz, ny, nx))
+    run = functools.partial(body, (nz, ny, nx), nz // 4 + 1)
     return jax.shard_map(
         run, mesh=mesh, in_specs=in_specs, out_specs=P(None, both, None), check_vma=False
     )

time: 47.3 us -> 36.6 us (0.77)
  Pallas kernels: 45.1 us -> 34.4 us
    pallas_call x1, Pallas kernels: 45.1 us -> 34.4 us  [body(): pl.pallas_call(functools.partial(kernel, dims, ahead), out_shape=jax.Shap...]
where the time goes in v3:
time: 36.6 us; the launch traced here: 36.4 us
  Pallas kernels  34.4 us (94%)
  local copies, waits for them, and re-layouts  1.35 us (4%)
  between operations  0.66 us (2%)
    pallas_call x1, Pallas kernels, body(): pl.pallas_call(functools.partial(kernel, dims, ahead), out_shape=jax.Shap...  34.4 us
    unnamed x1, local copies, waits for them, and re-layouts  1.35 us

profile of v3, /device:TPU:1, one launch (start us, length us, event | category | flops | bytes accessed | tf_op | source)
XLA Modules:
  0.0 36.4 jit_solution(8922154827744080340)
XLA Ops:
  0.7 34.4 %fmm.1 = f32[3,16,128]{2,1,0:T(8,128)} custom-call(f32[3,16,128]{2,1,0:T(8,128)} %pos_hbm.1, f32[3,16,128]{2,1,0:T(8,128)} %den_hbm.1, s32[16,12]{1,0:T(8,128)} %off_hbm.1, s32[16]{0:T(128)} %cnt_hbm.1, s32[1,189]{1,0:T(1,128)} %ids_hbm.1, s32[1,189]{1,0:T(1,128)} %ops_hbm.1, s32[1]{0:T(128)S(6)} %copy.13.lat_idx_hbm, bf16[512,384]{1,0:T(8,128)(2,1)} %up_hbm.1, ...), custom_call_target="tpu_custom_call" | custom-call | tf_op jit(solution)/shard_map/fmm/pallas_call | solution.py:423
  35.0 1.3 %copy.14 = f32[3,16,128]{2,1,0:T(8,128)} copy(f32[3,16,128]{2,1,0:T(8,128)} %fmm.1) | data formatting | bytes 49152

commit v4 on v3

--- a/solution.py
+++ b/solution.py
@@ -343,6 +343,14 @@
     z_wait(nz - quarter + 1, nz)
     forward(0)
 
+
+    share.wait_recv()
+    selector = jnp.concatenate([own_counts, crecv[...]], axis=0).astype(BF16)
+    for load in loads[7:]:
+        load.wait()
+
+    z_wait(quarter + 1, nz - quarter + 1)
+    forward(1)
     for copy in halos:
         copy.wait_recv()
     source_rows(0, [halo[0, c, 6:8, :] for c in range(3)], [halo[1, c, 6:8, :] for c in range(3)])
@@ -357,14 +365,6 @@
     scale = 1.0 / (8.0 * math.pi)
     lever = acc_s[:, 3, :]
     near_part = [(acc_s[:, c, :] + x[c] * lever) * scale for c in range(3)]
-
-    share.wait_recv()
-    selector = jnp.concatenate([own_counts, crecv[...]], axis=0).astype(BF16)
-    for load in loads[7:]:
-        load.wait()
-
-    z_wait(quarter + 1, nz - quarter + 1)
-    forward(1)
 
     def gathered(part):
         @pl.loop(1, planes)

time: 36.6 us -> 35.2 us (0.962)
  Pallas kernels: 34.4 us -> 33 us
    pallas_call x1, Pallas kernels: 34.4 us -> 33 us  [body(): pl.pallas_call(functools.partial(kernel, dims, ahead), out_shape=jax.Shap...]
where the time goes in v4:
time: 35.2 us; the launch traced here: 35 us
  Pallas kernels  33 us (94%)
  local copies, waits for them, and re-layouts  1.35 us (4%)
  between operations  0.66 us (2%)
    pallas_call x1, Pallas kernels, body(): pl.pallas_call(functools.partial(kernel, dims, ahead), out_shape=jax.Shap...  33 us
    unnamed x1, local copies, waits for them, and re-layouts  1.35 us

profile of v4, /device:TPU:1, one launch (start us, length us, event | category | flops | bytes accessed | tf_op | source)
XLA Modules:
  0.0 35.0 jit_solution(3006651343092366875)
XLA Ops:
  0.7 33.0 %fmm.1 = f32[3,16,128]{2,1,0:T(8,128)} custom-call(f32[3,16,128]{2,1,0:T(8,128)} %pos_hbm.1, f32[3,16,128]{2,1,0:T(8,128)} %den_hbm.1, s32[16,12]{1,0:T(8,128)} %off_hbm.1, s32[16]{0:T(128)} %cnt_hbm.1, s32[1,189]{1,0:T(1,128)} %ids_hbm.1, s32[1,189]{1,0:T(1,128)} %ops_hbm.1, s32[1]{0:T(128)S(6)} %copy.13.lat_idx_hbm, bf16[512,384]{1,0:T(8,128)(2,1)} %up_hbm.1, ...), custom_call_target="tpu_custom_call" | custom-call | tf_op jit(solution)/shard_map/fmm/pallas_call | solution.py:423
  33.7 1.3 %copy.14 = f32[3,16,128]{2,1,0:T(8,128)} copy(f32[3,16,128]{2,1,0:T(8,128)} %fmm.1) | data formatting | bytes 49152

commit v5 on v4

--- a/solution.py
+++ b/solution.py
@@ -325,13 +325,16 @@
         inner()
 
 
+    def hops(d):
+        up, along = d // nx, d % nx
+        return min(up, ny - up) + min(along, nx - along)
+
     def forward(part):
         for i in range(group):
             stage[i : i + 1, :] = gz[lax.rem(z + part * group + i - quarter + nz, nz)]
         plane[part, me_p] = stage[...].astype(BF16)
 
-        @pl.loop(1, planes)
-        def _(d):
+        for d in sorted(range(1, planes), key=hops, reverse=True):
             p_copy(part, d).start()
 
     def z_wait(lo, hi):

time: 35.2 us -> 34.8 us (0.989)
  Pallas kernels: 33 us -> 32.6 us
    pallas_call x1, Pallas kernels: 33 us -> 32.6 us  [body(): pl.pallas_call(functools.partial(kernel, dims, ahead), out_shape=jax.Shap...]
where the time goes in v5:
time: 34.8 us; the launch traced here: 34.6 us
  Pallas kernels  32.6 us (94%)
  local copies, waits for them, and re-layouts  1.35 us (4%)
  between operations  0.66 us (2%)
    pallas_call x1, Pallas kernels, body(): pl.pallas_call(functools.partial(kernel, dims, ahead), out_shape=jax.Shap...  32.6 us
    unnamed x1, local copies, waits for them, and re-layouts  1.35 us

profile of v5, /device:TPU:1, one launch (start us, length us, event | category | flops | bytes accessed | tf_op | source)
XLA Modules:
  0.0 34.6 jit_solution(14478198432500301187)
XLA Ops:
  0.7 32.6 %fmm.1 = f32[3,16,128]{2,1,0:T(8,128)} custom-call(f32[3,16,128]{2,1,0:T(8,128)} %pos_hbm.1, f32[3,16,128]{2,1,0:T(8,128)} %den_hbm.1, s32[16,12]{1,0:T(8,128)} %off_hbm.1, s32[16]{0:T(128)} %cnt_hbm.1, s32[1,189]{1,0:T(1,128)} %ids_hbm.1, s32[1,189]{1,0:T(1,128)} %ops_hbm.1, s32[1]{0:T(128)S(6)} %copy.13.lat_idx_hbm, bf16[512,384]{1,0:T(8,128)(2,1)} %up_hbm.1, ...), custom_call_target="tpu_custom_call" | custom-call | tf_op jit(solution)/shard_map/fmm/pallas_call | solution.py:426
  33.3 1.3 %copy.14 = f32[3,16,128]{2,1,0:T(8,128)} copy(f32[3,16,128]{2,1,0:T(8,128)} %fmm.1) | data formatting | bytes 49152
